TPU v7x, 32 devices: a whole 2x2x4 slice. The times are simulated.
32 devices in a mesh: shard: 8 (over z, x), seq: 4 (over y, core).
Axes of the slice: x: 2, y: 2, z: 4, core: 2. Of those that a mesh axis runs over, the one named last changes fastest.
Arguments:
- tokens: bfloat16 [16, 2048, 768], P('shard', 'seq'), may hold values from -6 to 6
- cotangent: bfloat16 [16, 2048, 768], P('shard', 'seq'), may hold values from -6 to 6
- query_weight: bfloat16 [768, 768], P('shard'), may hold values from -0.21875 to 0.21875
- key_weight: bfloat16 [768, 768], P('shard'), may hold values from -0.21875 to 0.21875
- value_weight: bfloat16 [768, 768], P('shard'), may hold values from -0.21875 to 0.21875
- output_weight: bfloat16 [768, 768], P('shard'), may hold values from -0.875 to 0.875
- inner_weight: bfloat16 [768, 3072], P('shard'), may hold values from -0.21875 to 0.21875
- inner_bias: bfloat16 [3072], P('shard'), may hold values from -3 to 3
- outer_weight: bfloat16 [3072, 768], P('shard'), may hold values from -0.109375 to 0.109375
- first_gain: bfloat16 [768], P('shard'), may hold values from 0.25 to 1.75
- first_shift: bfloat16 [768], P('shard'), may hold values from -3 to 3
- second_gain: bfloat16 [768], P('shard'), may hold values from 0.25 to 1.75
- second_shift: bfloat16 [768], P('shard'), may hold values from -3 to 3
- doc_starts: int32 [16, 3], P('shard'), may hold values from 0 to 2047, as said below
- random_blocks: int32 [16, 32, 3], P('shard'), may hold values from 0 to 31
Outputs:
- layer_output: bfloat16 [16, 2048, 768], P('shard', 'seq')
- input_grad: bfloat16 [16, 2048, 768], P('shard', 'seq')
- query_grad: float32 [768, 768], P('shard')
- key_grad: float32 [768, 768], P('shard')
- value_grad: float32 [768, 768], P('shard')
- projection_grad: float32 [768, 768], P('shard')
- inner_grad: float32 [768, 3072], P('shard')
- inner_bias_grad: float32 [3072], P('shard')
- outer_grad: float32 [3072, 768], P('shard')
- first_gain_grad: float32 [768], P('shard')
- first_shift_grad: float32 [768], P('shard')
- second_gain_grad: float32 [768], P('shard')
- second_shift_grad: float32 [768], P('shard')
Inputs may be any that keep to these rules, and one draw needn't show every extreme that they name: `doc_starts`: each sequence has 3 distinct starts in increasing order, the first 0, all below 2048; the last start of the first sequence is 2047.
All inputs are finite; a program needn't handle non-finite values.
Results may differ from a plain program's by a relative error of at most 0.017.
Values may be sent and summed in bfloat16 or wider, within the bound.
No kernel may reach another device: no remote copies, remote signals or barrier semaphores. Data moves between devices by JAX's collectives and lax.ppermute only.
A program may use at most 320 MiB of HBM per device.

v0:
```python
import math
import jax
import jax.numpy as jnp
from jax import lax
from jax.sharding import PartitionSpec as P

H = 12
HD = 64
BLK = 64
EPS = 1e-06


def for_sending(array):

    def short(part):
        return part.astype(jnp.bfloat16) if part.dtype == jnp.float32 else part

    return jax.tree.map(short, array)


def layer_norm(values, gain, shift):
    centered = values - jnp.mean(values, axis=-1, keepdims=True)
    spread = jnp.mean(centered * centered, axis=-1, keepdims=True)
    return centered * lax.rsqrt(spread + EPS) * gain + shift


def activate(values):
    return jax.nn.gelu(values, approximate=True)


def block_mask(starts, chosen, seq_len, width):
    blocks = seq_len // width
    places = jnp.arange(seq_len, dtype=jnp.int32)
    segment = jnp.sum((starts[None, :] <= places[:, None]).astype(jnp.int32), axis=1)
    follow = jnp.concatenate([starts[1:], jnp.full((1,), seq_len, jnp.int32)])
    first_block = starts // width
    last_block = (follow - 1) // width
    numbers = jnp.arange(blocks, dtype=jnp.int32)
    special = jnp.any(first_block[None, :] == numbers[:, None], axis=1) | jnp.any(
        last_block[None, :] == numbers[:, None], axis=1
    )
    nearby = jnp.abs(numbers[:, None] - numbers[None, :]) <= 1
    picked = jnp.any(chosen[:, :, None] == numbers[None, None, :], axis=1)
    blocked = nearby | special[:, None] | special[None, :] | picked
    expanded = jnp.repeat(jnp.repeat(blocked, width, axis=0), width, axis=1)
    return expanded & (segment[:, None] == segment[None, :])


def body(
    tokens,
    cotangent,
    query_weight,
    key_weight,
    value_weight,
    output_weight,
    inner_weight,
    inner_bias,
    outer_weight,
    first_gain,
    first_shift,
    second_gain,
    second_shift,
    doc_starts,
    random_blocks,
):
    gathered = (
        lax.all_gather(query_weight, "shard", axis=0, tiled=True),
        lax.all_gather(key_weight, "shard", axis=0, tiled=True),
        lax.all_gather(value_weight, "shard", axis=0, tiled=True),
        lax.all_gather(output_weight, "shard", axis=0, tiled=True),
        lax.all_gather(inner_weight, "shard", axis=0, tiled=True),
        lax.all_gather(inner_bias, "shard", axis=0, tiled=True),
        lax.all_gather(outer_weight, "shard", axis=0, tiled=True),
        lax.all_gather(first_gain, "shard", axis=0, tiled=True),
        lax.all_gather(first_shift, "shard", axis=0, tiled=True),
        lax.all_gather(second_gain, "shard", axis=0, tiled=True),
        lax.all_gather(second_shift, "shard", axis=0, tiled=True),
    )
    (
        query_full,
        key_full,
        value_full,
        output_full,
        inner_full,
        bias_full,
        outer_full,
        gain_one,
        shift_one,
        gain_two,
        shift_two,
    ) = gathered
    width = query_full.shape[0]
    hidden = inner_full.shape[1]
    joined_weight = jnp.concatenate([query_full, key_full, value_full], axis=1)
    bias_float = bias_full.astype(jnp.float32)
    gain_one_f = gain_one.astype(jnp.float32)
    shift_one_f = shift_one.astype(jnp.float32)
    gain_two_f = gain_two.astype(jnp.float32)
    shift_two_f = shift_two.astype(jnp.float32)
    groups = lax.axis_size("seq")
    local_len = tokens.shape[1]
    seq_len = local_len * groups
    head_group = H // groups
    group_width = head_group * HD
    block_rows = min(512, seq_len)
    scale = 1.0 / math.sqrt(HD)

    def micro_step(totals, inputs):
        (
            acc_joined,
            acc_output,
            acc_inner,
            acc_bias,
            acc_outer,
            acc_gain_one,
            acc_shift_one,
            acc_gain_two,
            acc_shift_two,
        ) = totals
        row, grad_row, starts, chosen = inputs
        attend = block_mask(starts, chosen, seq_len, BLK)
        joined = jnp.dot(row, joined_weight, preferred_element_type=jnp.float32).astype(
            jnp.bfloat16
        )
        joined = joined.reshape(local_len, 3, groups, group_width)
        by_heads = lax.all_to_all(joined, "seq", split_axis=2, concat_axis=0, tiled=True).reshape(
            seq_len, 3, head_group, HD
        )
        queries = by_heads[:, 0]
        keys_all = by_heads[:, 1]
        values_all = by_heads[:, 2]

        def masked_scores(start):
            query_block = queries[start : start + block_rows]
            scores = (
                jnp.einsum(
                    "qhd,khd->hqk", query_block, keys_all, preferred_element_type=jnp.float32
                )
                * scale
            )
            return (
                query_block,
                jnp.where(attend[start : start + block_rows][None], scores, -1000000000.0),
            )

        contexts = []
        log_totals = []
        for start in range(0, seq_len, block_rows):
            query_block, scores = masked_scores(start)
            highest_score = jnp.max(scores, axis=-1, keepdims=True)
            expd = jnp.exp(scores - highest_score)
            denom = jnp.sum(expd, axis=-1, keepdims=True)
            probs = expd / denom
            log_totals.append(highest_score + jnp.log(denom))
            contexts.append(
                jnp.einsum(
                    "hqk,khd->qhd",
                    probs.astype(jnp.bfloat16),
                    values_all,
                    preferred_element_type=jnp.float32,
                ).astype(jnp.bfloat16)
            )
        context_heads = jnp.concatenate(contexts, axis=0).reshape(seq_len, 1, group_width)
        context = (
            lax.all_to_all(
                for_sending(context_heads), "seq", split_axis=0, concat_axis=1, tiled=True
            )
            .astype(context_heads.dtype)
            .reshape(local_len, width)
        )
        attended = jnp.dot(context, output_full, preferred_element_type=jnp.float32)
        res_one = row.astype(jnp.float32) + attended
        first = layer_norm(res_one, gain_one_f, shift_one_f)
        first_low = first.astype(jnp.bfloat16)
        inner = jnp.dot(first_low, inner_full, preferred_element_type=jnp.float32) + bias_float
        active = activate(inner).astype(jnp.bfloat16)
        outer = jnp.dot(active, outer_full, preferred_element_type=jnp.float32)
        res_two = first + outer
        result = layer_norm(res_two, gain_two_f, shift_two_f).astype(jnp.bfloat16)
        grad_float = grad_row.astype(jnp.float32)
        _, norm_two_back = jax.vjp(layer_norm, res_two, gain_two_f, shift_two_f)
        d_second, d_gain_two, d_shift_two = norm_two_back(grad_float)
        d_outer = d_second.astype(jnp.bfloat16)
        acc_outer = acc_outer + jnp.einsum(
            "ti,td->id", active, d_outer, preferred_element_type=jnp.float32
        )
        d_active = jnp.einsum("td,id->ti", d_outer, outer_full, preferred_element_type=jnp.float32)
        _, gelu_back = jax.vjp(activate, inner)
        d_inner = gelu_back(d_active)[0].astype(jnp.bfloat16)
        acc_bias = acc_bias + jnp.sum(d_inner.astype(jnp.float32), axis=0)
        acc_inner = acc_inner + jnp.einsum(
            "td,tf->df", first_low, d_inner, preferred_element_type=jnp.float32
        )
        d_first = d_second + jnp.einsum(
            "tf,df->td", d_inner, inner_full, preferred_element_type=jnp.float32
        )
        _, norm_one_back = jax.vjp(layer_norm, res_one, gain_one_f, shift_one_f)
        d_res, d_gain_one, d_shift_one = norm_one_back(d_first)
        d_attended = d_res.astype(jnp.bfloat16)
        acc_output = acc_output + jnp.einsum(
            "ti,td->id", context, d_attended, preferred_element_type=jnp.float32
        )
        d_context = jnp.einsum(
            "td,id->ti", d_attended, output_full, preferred_element_type=jnp.float32
        )
        d_context = d_context.astype(jnp.bfloat16).reshape(local_len, groups, group_width)
        d_heads = lax.all_to_all(d_context, "seq", split_axis=1, concat_axis=0, tiled=True).reshape(
            seq_len, head_group, HD
        )
        d_keys = jnp.zeros((seq_len, head_group, HD), jnp.float32)
        d_values = jnp.zeros((seq_len, head_group, HD), jnp.float32)
        d_query_blocks = []
        for index, start in enumerate(range(0, seq_len, block_rows)):
            query_block, scores = masked_scores(start)
            probs = jnp.exp(scores - log_totals[index])
            grad_block = d_heads[start : start + block_rows]
            d_probs = jnp.einsum(
                "qhd,khd->hqk", grad_block, values_all, preferred_element_type=jnp.float32
            )
            d_values = d_values + jnp.einsum(
                "hqk,qhd->khd",
                probs.astype(jnp.bfloat16),
                grad_block,
                preferred_element_type=jnp.float32,
            )
            centered = d_probs - jnp.sum(probs * d_probs, axis=-1, keepdims=True)
            d_scores = (probs * centered * scale).astype(jnp.bfloat16)
            d_query_blocks.append(
                jnp.einsum("hqk,khd->qhd", d_scores, keys_all, preferred_element_type=jnp.float32)
            )
            d_keys = d_keys + jnp.einsum(
                "hqk,qhd->khd", d_scores, query_block, preferred_element_type=jnp.float32
            )
        d_queries = jnp.concatenate(d_query_blocks, axis=0)
        d_joined = jnp.stack([d_queries, d_keys, d_values], axis=1).astype(jnp.bfloat16)
        d_joined = d_joined.reshape(seq_len, 3, 1, group_width)
        d_local = lax.all_to_all(d_joined, "seq", split_axis=0, concat_axis=2, tiled=True).reshape(
            local_len, 3 * width
        )
        acc_joined = acc_joined + jnp.einsum(
            "td,te->de", row, d_local, preferred_element_type=jnp.float32
        )
        d_input = d_res + jnp.einsum(
            "te,de->td", d_local, joined_weight, preferred_element_type=jnp.float32
        )
        updated = (
            acc_joined,
            acc_output,
            acc_inner,
            acc_bias,
            acc_outer,
            acc_gain_one + d_gain_one,
            acc_shift_one + d_shift_one,
            acc_gain_two + d_gain_two,
            acc_shift_two + d_shift_two,
        )
        return (updated, (result, d_input.astype(jnp.bfloat16)))

    starting = (
        jnp.zeros((width, 3 * width), jnp.float32),
        jnp.zeros((width, width), jnp.float32),
        jnp.zeros((width, hidden), jnp.float32),
        jnp.zeros((hidden,), jnp.float32),
        jnp.zeros((hidden, width), jnp.float32),
        jnp.zeros((width,), jnp.float32),
        jnp.zeros((width,), jnp.float32),
        jnp.zeros((width,), jnp.float32),
        jnp.zeros((width,), jnp.float32),
    )
    totals, (outputs, input_grads) = lax.scan(
        micro_step, starting, (tokens, cotangent, doc_starts, random_blocks)
    )
    (
        acc_joined,
        acc_output,
        acc_inner,
        acc_bias,
        acc_outer,
        acc_gain_one,
        acc_shift_one,
        acc_gain_two,
        acc_shift_two,
    ) = totals
    local_grads = (
        acc_joined[:, :width],
        acc_joined[:, width : 2 * width],
        acc_joined[:, 2 * width :],
        acc_output,
        acc_inner,
        acc_bias,
        acc_outer,
        acc_gain_one,
        acc_shift_one,
        acc_gain_two,
        acc_shift_two,
    )
    shares = (
        lax.psum_scatter(local_grads[0], "shard", scatter_dimension=0, tiled=True),
        lax.psum_scatter(local_grads[1], "shard", scatter_dimension=0, tiled=True),
        lax.psum_scatter(local_grads[2], "shard", scatter_dimension=0, tiled=True),
        lax.psum_scatter(local_grads[3], "shard", scatter_dimension=0, tiled=True),
        lax.psum_scatter(local_grads[4], "shard", scatter_dimension=0, tiled=True),
        lax.psum_scatter(local_grads[5], "shard", scatter_dimension=0, tiled=True),
        lax.psum_scatter(local_grads[6], "shard", scatter_dimension=0, tiled=True),
        lax.psum_scatter(local_grads[7], "shard", scatter_dimension=0, tiled=True),
        lax.psum_scatter(local_grads[8], "shard", scatter_dimension=0, tiled=True),
        lax.psum_scatter(local_grads[9], "shard", scatter_dimension=0, tiled=True),
        lax.psum_scatter(local_grads[10], "shard", scatter_dimension=0, tiled=True),
    )
    summed = (
        lax.psum(shares[0].astype(jnp.bfloat16), "seq").astype(jnp.float32),
        lax.psum(shares[1].astype(jnp.bfloat16), "seq").astype(jnp.float32),
        lax.psum(shares[2].astype(jnp.bfloat16), "seq").astype(jnp.float32),
        lax.psum(shares[3].astype(jnp.bfloat16), "seq").astype(jnp.float32),
        lax.psum(shares[4].astype(jnp.bfloat16), "seq").astype(jnp.float32),
        lax.psum(shares[5].astype(jnp.bfloat16), "seq").astype(jnp.float32),
        lax.psum(shares[6].astype(jnp.bfloat16), "seq").astype(jnp.float32),
        lax.psum(shares[7].astype(jnp.bfloat16), "seq").astype(jnp.float32),
        lax.psum(shares[8].astype(jnp.bfloat16), "seq").astype(jnp.float32),
        lax.psum(shares[9].astype(jnp.bfloat16), "seq").astype(jnp.float32),
        lax.psum(shares[10].astype(jnp.bfloat16), "seq").astype(jnp.float32),
    )
    return (
        outputs,
        input_grads,
        summed[0],
        summed[1],
        summed[2],
        summed[3],
        summed[4],
        summed[5],
        summed[6],
        summed[7],
        summed[8],
        summed[9],
        summed[10],
    )


def solution(mesh):
    placed = (
        P("shard", "seq", None),
        P("shard", "seq", None),
        P("shard", None),
        P("shard", None),
        P("shard", None),
        P("shard", None),
        P("shard", None),
        P("shard"),
        P("shard", None),
        P("shard"),
        P("shard"),
        P("shard"),
        P("shard"),
        P("shard", None),
        P("shard", None, None),
    )
    return jax.shard_map(
        body,
        mesh=mesh,
        in_specs=placed,
        out_specs=(
            P("shard", "seq", None),
            P("shard", "seq", None),
            P("shard", None),
            P("shard", None),
            P("shard", None),
            P("shard", None),
            P("shard", None),
            P("shard"),
            P("shard", None),
            P("shard"),
            P("shard"),
            P("shard"),
            P("shard"),
        ),
        check_vma=False,
    )
```

profile of v0, /device:TPU:0, one launch (start us, length us, event | category | flops | bytes accessed | tf_op | source)
XLA Modules:
  0.0 2124.0 jit_solution(12101311446130389150)
XLA Ops:
  41.4 26.0 %all-gather = bf16[8,1,384]{2,1,0:T(2,128)(2,1)S(1)} all-gather(bf16[1,1,384]{2,1,0:T(2,128)(2,1)S(1)} %reshape.380), channel_id=1, replica_groups=mesh['shard'=8,'seq'=4] {'shard'}, dimensions={0}, use_global_device_ids=true | all-gather | bytes 6912 | tf_op jit(solution)/shard_map/all_gather | solution.py:72
  67.5 28.6 %all-gather.10.cloned.1.call-done = bf16[768,768]{1,0:T(8,128)(2,1)} async-done(((bf16[96,768]{1,0:T(8,128)(2,1)}), bf16[768,768]{1,0:T(8,128)(2,1)}) %all-gather.10.cloned.1.call-update) | async-done | bytes 1179664 | tf_op jit(solution)/shard_map/all_gather | solution.py:68
  96.1 42.0 %all-gather.12.cloned.1.call-done = bf16[768,768]{1,0:T(8,128)(2,1)} async-done(((bf16[96,768]{1,0:T(8,128)(2,1)}), bf16[768,768]{1,0:T(8,128)(2,1)}) %all-gather.12.cloned.1.call-update) | async-done | bytes 1179664 | tf_op jit(solution)/shard_map/all_gather | solution.py:69
  141.4 38.6 %all-gather.14.cloned.1.call-done = bf16[768,768]{1,0:T(8,128)(2,1)} async-done(((bf16[96,768]{1,0:T(8,128)(2,1)}), bf16[768,768]{1,0:T(8,128)(2,1)}) %all-gather.14.cloned.1.call-update) | async-done | bytes 1179664 | tf_op jit(solution)/shard_map/all_gather | solution.py:70
  180.0 80.1 %all-gather.16.cloned.1.call-done = bf16[768,3072]{1,0:T(8,128)(2,1)} async-done(((bf16[96,3072]{1,0:T(8,128)(2,1)}), bf16[768,3072]{1,0:T(8,128)(2,1)}) %all-gather.16.cloned.1.call-update) | async-done | bytes 4718608 | tf_op jit(solution)/shard_map/all_gather | solution.py:71
  260.1 79.8 %all-gather.18.cloned.1.call-done = bf16[3072,768]{1,0:T(8,128)(2,1)} async-done(((bf16[384,768]{1,0:T(8,128)(2,1)}), bf16[3072,768]{1,0:T(8,128)(2,1)}) %all-gather.18.cloned.1.call-update) | async-done | bytes 4718608 | tf_op jit(solution)/shard_map/all_gather | solution.py:73
  339.8 1103.4 %while.34 = (s32[]{:T(128)}, f32[768,2304]{1,0:T(8,128)}, f32[768,768]{1,0:T(8,128)}, f32[768,3072]{1,0:T(8,128)}, f32[3072]{0:T(1024)}, /*index=5*/f32[3072,768...) while((s32[]{:T(128)}, f32[768,2304]{1,0:T(8,128)}, ...), condition=%wide.region_30.31_spmd.clone, body=%wide.region_0.30_spmd.clone.sunk | while | flops 32024104960 | bytes 1287496960 | solution.py:270
  573.9 27.8 %fusion.472 = f32[3,64,2048]{2,1,0:T(8,128)} fusion(f32[3,512,2048]{2,1,0:T(8,128)} %fusion.471, f32[3,512,2048]{2,1,0:T(8,128)} %get-tuple-element.919, f32[3,512]{1,0:T(4,128)S(1)} %log_add_fusion.10, pred[512,2048]{1,0:T(8,128)(4,1)} %copy.126, bf16[2048,3,3,64]{0,3,2,1:T(8,128)(2,1)S(1)} %copy-done.2), kind=kOutput, calls=%fused_computation.47.clone.1 | convolution fusion | flops 437259776 | bytes 54214656 | tf_op jit(solution)/shard_map/while/body/eval_jaxpr/hqk,qhd->khd/dot_general | solution.py:231
  669.8 23.9 %fusion.480 = bf16[512,3,64]{0,2,1:T(8,128)(2,1)} fusion(f32[3,512,2048]{2,1,0:T(8,128)} %fusion.475, f32[3,512,2048]{2,1,0:T(8,128)} %get-tuple-element.913, f32[3,512]{1,0:T(4,128)S(1)} %log_add_fusion.8, pred[512,2048]{1,0:T(8,128)(4,1)} %copy.124, bf16[2048,3,3,64]{0,3,2,1:T(8,128)(2,1)S(1)} %copy-done.2), kind=kOutput, calls=%fused_computation.158.clone.1 | convolution fusion | flops 437358080 | bytes 53428224 | tf_op jit(solution)/shard_map/while/body/eval_jaxpr/hqk,khd->qhd/dot_general | solution.py:229
  693.7 24.0 %fusion.481 = bf16[512,3,64]{0,2,1:T(8,128)(2,1)} fusion(f32[3,512,2048]{2,1,0:T(8,128)} %fusion.473, f32[3,512,2048]{2,1,0:T(8,128)} %get-tuple-element.916, f32[3,512]{1,0:T(4,128)S(1)} %log_add_fusion.9, pred[512,2048]{1,0:T(8,128)(4,1)} %copy.125, bf16[2048,3,3,64]{0,3,2,1:T(8,128)(2,1)S(1)} %copy-done.2), kind=kOutput, calls=%fused_computation.157.clone.1 | convolution fusion | flops 437358080 | bytes 53428224 | tf_op jit(solution)/shard_map/while/body/eval_jaxpr/hqk,khd->qhd/dot_general | solution.py:229
  717.7 25.7 %fusion.474 = f32[3,64,2048]{2,1,0:T(8,128)} fusion(f32[3,64,2048]{2,1,0:T(8,128)} %fusion.472, f32[3,512,2048]{2,1,0:T(8,128)} %fusion.473, f32[3,512,2048]{2,1,0:T(8,128)} %get-tuple-element.916, f32[3,512]{1,0:T(4,128)S(1)} %log_add_fusion.9, pred[512,2048]{1,0:T(8,128)(4,1)} %copy.125, bf16[2048,3,3,64]{0,3,2,1:T(8,128)(2,1)S(1)} %copy-done.2), kind=kOutput, calls=%fused_computation.118.clone.1 | convolution fusion | flops 437652992 | bytes 55787520 | tf_op jit(solution)/shard_map/while/body/eval_jaxpr/hqk,qhd->khd/dot_general | solution.py:231
  743.4 26.0 %fusion.476 = f32[3,64,2048]{2,1,0:T(8,128)} fusion(f32[3,64,2048]{2,1,0:T(8,128)} %fusion.474, f32[3,512,2048]{2,1,0:T(8,128)} %fusion.475, f32[3,512,2048]{2,1,0:T(8,128)} %get-tuple-element.913, f32[3,512]{1,0:T(4,128)S(1)} %log_add_fusion.8, pred[512,2048]{1,0:T(8,128)(4,1)} %copy.124, bf16[2048,3,3,64]{0,3,2,1:T(8,128)(2,1)S(1)} %copy-done.2), kind=kOutput, calls=%fused_computation.117.clone.1 | convolution fusion | flops 437652992 | bytes 55787520 | tf_op jit(solution)/shard_map/while/body/eval_jaxpr/hqk,qhd->khd/dot_general | solution.py:231
  830.7 35.7 %all-to-all-done.3 = bf16[2048,3,1,192]{3,1,2,0:T(4,128)(2,1)} async-done(((bf16[2048,3,1,192]{3,1,2,0:T(4,128)(2,1)}), bf16[2048,3,1,192]{3,1,2,0:T(4,128)(2,1)}, u32[]{:S(2)}, u32[]{:S(2)}) %all-to-all-start.3) | async-done | bytes 2359328 | tf_op jit(solution)/shard_map/while/body/eval_jaxpr/all_to_all | solution.py:237
  1124.3 28.0 %fusion.472 = f32[3,64,2048]{2,1,0:T(8,128)} fusion(f32[3,512,2048]{2,1,0:T(8,128)} %fusion.471, f32[3,512,2048]{2,1,0:T(8,128)} %get-tuple-element.919, f32[3,512]{1,0:T(4,128)S(1)} %log_add_fusion.10, pred[512,2048]{1,0:T(8,128)(4,1)} %copy.126, bf16[2048,3,3,64]{0,3,2,1:T(8,128)(2,1)S(1)} %copy-done.2), kind=kOutput, calls=%fused_computation.47.clone.1 | convolution fusion | flops 437259776 | bytes 54214656 | tf_op jit(solution)/shard_map/while/body/eval_jaxpr/hqk,qhd->khd/dot_general | solution.py:231
  1268.2 25.7 %fusion.474 = f32[3,64,2048]{2,1,0:T(8,128)} fusion(f32[3,64,2048]{2,1,0:T(8,128)} %fusion.472, f32[3,512,2048]{2,1,0:T(8,128)} %fusion.473, f32[3,512,2048]{2,1,0:T(8,128)} %get-tuple-element.916, f32[3,512]{1,0:T(4,128)S(1)} %log_add_fusion.9, pred[512,2048]{1,0:T(8,128)(4,1)} %copy.125, bf16[2048,3,3,64]{0,3,2,1:T(8,128)(2,1)S(1)} %copy-done.2), kind=kOutput, calls=%fused_computation.118.clone.1 | convolution fusion | flops 437652992 | bytes 55787520 | tf_op jit(solution)/shard_map/while/body/eval_jaxpr/hqk,qhd->khd/dot_general | solution.py:231
  1293.9 26.0 %fusion.476 = f32[3,64,2048]{2,1,0:T(8,128)} fusion(f32[3,64,2048]{2,1,0:T(8,128)} %fusion.474, f32[3,512,2048]{2,1,0:T(8,128)} %fusion.475, f32[3,512,2048]{2,1,0:T(8,128)} %get-tuple-element.913, f32[3,512]{1,0:T(4,128)S(1)} %log_add_fusion.8, pred[512,2048]{1,0:T(8,128)(4,1)} %copy.124, bf16[2048,3,3,64]{0,3,2,1:T(8,128)(2,1)S(1)} %copy-done.2), kind=kOutput, calls=%fused_computation.117.clone.1 | convolution fusion | flops 437652992 | bytes 55787520 | tf_op jit(solution)/shard_map/while/body/eval_jaxpr/hqk,qhd->khd/dot_general | solution.py:231
  1385.8 31.3 %all-to-all-done.3 = bf16[2048,3,1,192]{3,1,2,0:T(4,128)(2,1)} async-done(((bf16[2048,3,1,192]{3,1,2,0:T(4,128)(2,1)}), bf16[2048,3,1,192]{3,1,2,0:T(4,128)(2,1)}, u32[]{:S(2)}, u32[]{:S(2)}) %all-to-all-start.3) | async-done | bytes 2359328 | tf_op jit(solution)/shard_map/while/body/eval_jaxpr/all_to_all | solution.py:237
  1452.2 58.3 %reduce-scatter.13.cloned.1.call-done = f32[96,768]{1,0:T(8,128)} async-done(((f32[768,768]{1,0:T(8,128)}), f32[96,768]{1,0:T(8,128)}) %reduce-scatter.13.cloned.1.call-update) | async-done | bytes 294928 | tf_op jit(solution)/shard_map/reduce_scatter | solution.py:301
  1512.1 70.6 %reduce-scatter.11.cloned.1.call-done = f32[96,768]{1,0:T(8,128)} async-done(((f32[768,768]{1,0:T(8,128)}), f32[96,768]{1,0:T(8,128)}) %reduce-scatter.11.cloned.1.call-update) | async-done | bytes 294928 | tf_op jit(solution)/shard_map/reduce_scatter | solution.py:300
  1584.4 70.7 %reduce-scatter.7.cloned.1.call-done = f32[96,768]{1,0:T(8,128)} async-done(((f32[768,768]{1,0:T(8,128)}), f32[96,768]{1,0:T(8,128)}) %reduce-scatter.7.cloned.1.call-update) | async-done | bytes 294928 | tf_op jit(solution)/shard_map/reduce_scatter | solution.py:298
  1656.7 70.5 %reduce-scatter.9.cloned.1.call-done = f32[96,768]{1,0:T(8,128)} async-done(((f32[768,768]{1,0:T(8,128)}), f32[96,768]{1,0:T(8,128)}) %reduce-scatter.9.cloned.1.call-update) | async-done | bytes 294928 | tf_op jit(solution)/shard_map/reduce_scatter | solution.py:299
  1728.9 163.3 %reduce-scatter.15.cloned.1.call-done = f32[96,3072]{1,0:T(8,128)} async-done(((f32[768,3072]{1,0:T(8,128)}), f32[96,3072]{1,0:T(8,128)}) %reduce-scatter.15.cloned.1.call-update) | async-done | bytes 1179664 | tf_op jit(solution)/shard_map/reduce_scatter | solution.py:302
  1894.3 162.5 %reduce-scatter.17.cloned.1.call-done = f32[384,768]{1,0:T(8,128)} async-done(((f32[3072,768]{1,0:T(8,128)}), f32[384,768]{1,0:T(8,128)}) %reduce-scatter.17.cloned.1.call-update) | async-done | bytes 1179664 | tf_op jit(solution)/shard_map/reduce_scatter | solution.py:304
  2060.4 35.2 %all-reduce.9 = (bf16[3072]{0:T(1024)(128)(2,1)S(1)}, bf16[768]{0:T(1024)(128)(2,1)S(1)}, bf16[768]{0:T(1024)(128)(2,1)S(1)}, bf16[768]{0:T(1024)(128)(2,1)S(1)}, bf16[768]{0:T(1024)(128)(2,1)S(1)}) all-reduce(f32[3072]{0:T(1024)S(1)} %copy-done.26, f32[768]{0:T(1024)S(1)} %copy-done.40, ...), channel_id=7, replica_groups=mesh['shard'=8,'seq'=4] {'shard'}, use_global_device_ids=true, to_apply=%region_41.42.clone | all-reduce | flops 6144 | bytes 36864
  (514 shorter events, 902.6 us)
Async XLA Ops:
  7.2 60.3 %all-gather.8.cloned.1.call-start = ((), (), s32[]{:S(2)}) async-start(), calls=%async_computation.10 | async-start | bytes 1327104 | tf_op jit(solution)/shard_map/all_gather | solution.py:67
  7.9 88.2 %all-gather.10.cloned.1.call-start = ((), (), s32[]{:S(2)}) async-start(), calls=%async_computation.11 | async-start | bytes 1327104 | tf_op jit(solution)/shard_map/all_gather | solution.py:68
  8.7 129.4 %all-gather.12.cloned.1.call-start = ((), (), s32[]{:S(2)}) async-start(), calls=%async_computation.12 | async-start | bytes 1327104 | tf_op jit(solution)/shard_map/all_gather | solution.py:69
  9.4 170.6 %all-gather.14.cloned.1.call-start = ((), (), s32[]{:S(2)}) async-start(), calls=%async_computation.13 | async-start | bytes 1327104 | tf_op jit(solution)/shard_map/all_gather | solution.py:70
  10.0 250.1 %all-gather.16.cloned.1.call-start = ((), (), s32[]{:S(2)}) async-start(), calls=%async_computation.14 | async-start | bytes 5308416 | tf_op jit(solution)/shard_map/all_gather | solution.py:71
  10.6 329.3 %all-gather.18.cloned.1.call-start = ((), (), s32[]{:S(2)}) async-start(), calls=%async_computation.15 | async-start | bytes 5308416 | tf_op jit(solution)/shard_map/all_gather | solution.py:73
  11.1 1499.4 %reduce-scatter.13.cloned.1.call-start = ((), (), s32[]{:S(2)}) async-start(), calls=%async_computation.19 | async-start | bytes 2654208 | tf_op jit(solution)/shard_map/reduce_scatter | solution.py:301
  350.1 32.1 %all-to-all-start = ((bf16[512,3,4,192]{0,3,1,2:T(8,128)(2,1)}), bf16[512,3,4,192]{0,3,1,2:T(8,128)(2,1)S(1)}, u32[]{:S(2)}, u32[]{:S(2)}) async-start(bf16[512,3,4,192]{0,3,1,2:T(8,128)(2,1)} %copy.122), calls=%async_computation | async-start | bytes 4718592 | tf_op jit(solution)/shard_map/while/body/eval_jaxpr/all_to_all | solution.py:126
  474.8 15.1 all-to-all-start.1
  524.8 15.9 all-to-all-start.2
  813.0 53.4 %all-to-all-start.3 = ((bf16[2048,3,1,192]{3,1,2,0:T(4,128)(2,1)}), bf16[2048,3,1,192]{3,1,2,0:T(4,128)(2,1)}, u32[]{:S(2)}, u32[]{:S(2)}) async-start(bf16[2048,3,1,192]{3,1,2,0:T(4,128)(2,1)} %pad_maximum_fusion.9), calls=%async_computation.3 | async-start | bytes 8388608 | tf_op jit(solution)/shard_map/while/body/eval_jaxpr/all_to_all | solution.py:237
  900.7 32.1 %all-to-all-start = ((bf16[512,3,4,192]{0,3,1,2:T(8,128)(2,1)}), bf16[512,3,4,192]{0,3,1,2:T(8,128)(2,1)S(1)}, u32[]{:S(2)}, u32[]{:S(2)}) async-start(bf16[512,3,4,192]{0,3,1,2:T(8,128)(2,1)} %copy.122), calls=%async_computation | async-start | bytes 4718592 | tf_op jit(solution)/shard_map/while/body/eval_jaxpr/all_to_all | solution.py:126
  1025.4 15.1 all-to-all-start.1
  1075.3 15.9 all-to-all-start.2
  1363.7 53.3 %all-to-all-start.3 = ((bf16[2048,3,1,192]{3,1,2,0:T(4,128)(2,1)}), bf16[2048,3,1,192]{3,1,2,0:T(4,128)(2,1)}, u32[]{:S(2)}, u32[]{:S(2)}) async-start(bf16[2048,3,1,192]{3,1,2,0:T(4,128)(2,1)} %pad_maximum_fusion.9), calls=%async_computation.3 | async-start | bytes 8388608 | tf_op jit(solution)/shard_map/while/body/eval_jaxpr/all_to_all | solution.py:237
  1443.2 139.6 %reduce-scatter.11.cloned.1.call-start = ((), (), s32[]{:S(2)}) async-start(), calls=%async_computation.18 | async-start | bytes 2654208 | tf_op jit(solution)/shard_map/reduce_scatter | solution.py:300
  1449.5 205.6 %reduce-scatter.7.cloned.1.call-start = ((), (), s32[]{:S(2)}) async-start(), calls=%async_computation.16 | async-start | bytes 2654208 | tf_op jit(solution)/shard_map/reduce_scatter | solution.py:298
  1450.3 277.0 %reduce-scatter.9.cloned.1.call-start = ((), (), s32[]{:S(2)}) async-start(), calls=%async_computation.17 | async-start | bytes 2654208 | tf_op jit(solution)/shard_map/reduce_scatter | solution.py:299
  1450.8 441.3 %reduce-scatter.15.cloned.1.call-start = ((), (), s32[]{:S(2)}) async-start(), calls=%async_computation.20 | async-start | bytes 10616832 | tf_op jit(solution)/shard_map/reduce_scatter | solution.py:302
  1451.6 605.3 %reduce-scatter.17.cloned.1.call-start = ((), (), s32[]{:S(2)}) async-start(), calls=%async_computation.21 | async-start | bytes 10616832 | tf_op jit(solution)/shard_map/reduce_scatter | solution.py:304
  1451.6 608.7 %copy-start.26 = (f32[3072]{0:T(1024)S(1)}, f32[3072]{0:T(1024)}, u32[]{:S(2)}) copy-start(f32[3072]{0:T(1024)} %get-tuple-element.396) | copy-start | bytes 36868
  1451.6 608.7 %copy-start.31 = (f32[768]{0:T(1024)S(1)}, f32[768]{0:T(1024)}, u32[]{:S(2)}) copy-start(f32[768]{0:T(1024)} %get-tuple-element.401) | copy-start | bytes 9220
  1451.6 608.7 %copy-start.34 = (f32[768]{0:T(1024)S(1)}, f32[768]{0:T(1024)}, u32[]{:S(2)}) copy-start(f32[768]{0:T(1024)} %get-tuple-element.400) | copy-start | bytes 9220
  1452.2 654.1 %all-reduce.15.cloned.1.call-start = ((), (), s32[]{:S(2)}) async-start(), calls=%async_computation.22 | async-start | bytes 3538944 | tf_op jit(solution)/shard_map/psum | solution.py:311
  (102 other events, 2472.0 us)
Sparse Core Ops, SparseCore 0:
  10.2 43.8 all-gather.7
  56.2 39.8 all-gather.9
  98.3 39.8 all-gather.11
  140.1 39.8 all-gather.13
  182.0 78.0 all-gather.15
  262.1 77.6 all-gather.17
  1443.3 67.1 reduce-scatter.12
  1514.0 68.7 reduce-scatter.10
  1586.3 68.7 reduce-scatter.6
  1658.4 68.7 reduce-scatter.8
  1730.8 161.3 reduce-scatter.14
  1895.6 161.1 reduce-scatter.16
  2060.8 45.3 all-reduce.14
where the time goes:
time: 2130 us; the launch traced here: 2120 us
  waiting for transfers between devices  973 us (46%)
  matrix products  720 us (34%)
  local copies, waits for them, and re-layouts  156 us (7%)
  other arithmetic  130 us (6%)
  blocking collectives  91.2 us (4%)
  starting transfers between devices  33.5 us (2%)
    dot_general x8, matrix products, micro_step(): jnp.einsum('hqk,qhd->khd', d_scores, query_block, preferred_element_type=...  204 us
    dot_general x8, matrix products, micro_step(): jnp.einsum('hqk,khd->qhd', d_scores, keys_all, preferred_element_type=jnp...  184 us
    reduce_scatter x1, waiting for transfers between devices, body(): lax.psum_scatter(local_grads[4], 'shard', scatter_dimension=0, tiled=True)  163 us
    reduce_scatter x1, waiting for transfers between devices, body(): lax.psum_scatter(local_grads[6], 'shard', scatter_dimension=0, tiled=True)  163 us
    all_gather x1, waiting for transfers between devices, body(): lax.all_gather(inner_weight, 'shard', axis=0, tiled=True)  80.1 us
    all_gather x1, waiting for transfers between devices, body(): lax.all_gather(outer_weight, 'shard', axis=0, tiled=True)  79.8 us
    reduce_scatter x1, waiting for transfers between devices, body(): lax.psum_scatter(local_grads[0], 'shard', scatter_dimension=0, tiled=True)  70.7 us
    reduce_scatter x1, waiting for transfers between devices, body(): lax.psum_scatter(local_grads[2], 'shard', scatter_dimension=0, tiled=True)  70.6 us
  transfers between devices with their start and end apart: 21, of which 20 were waited for; matrix products, arithmetic and copies ran while one was open for 6% of the time, Pallas kernels for 0%

commit v1 on v0

--- a/solution.py
+++ b/solution.py
@@ -8,6 +8,13 @@
 HD = 64
 BLK = 64
 EPS = 1e-06
+
+
+def trade_parts(value, mesh_axis, split, join):
+    count = lax.axis_size(mesh_axis)
+    blocks = jnp.stack(jnp.split(value, count, axis=split), axis=0)
+    blocks = lax.all_to_all(blocks, mesh_axis, split_axis=0, concat_axis=0)
+    return jnp.concatenate(blocks, axis=join)
 
 
 def for_sending(array):
@@ -234,9 +241,7 @@
         d_queries = jnp.concatenate(d_query_blocks, axis=0)
         d_joined = jnp.stack([d_queries, d_keys, d_values], axis=1).astype(jnp.bfloat16)
         d_joined = d_joined.reshape(seq_len, 3, 1, group_width)
-        d_local = lax.all_to_all(d_joined, "seq", split_axis=0, concat_axis=2, tiled=True).reshape(
-            local_len, 3 * width
-        )
+        d_local = trade_parts(d_joined, "seq", 0, 2).reshape(local_len, 3 * width)
         acc_joined = acc_joined + jnp.einsum(
             "td,te->de", row, d_local, preferred_element_type=jnp.float32
         )

time: 2130 us -> 2020 us (0.948)
  local copies, waits for them, and re-layouts: 156 us -> 101 us
  waiting for transfers between devices: 973 us -> 931 us
    all_to_all x2, waiting for transfers between devices: 67 us -> 25.6 us  [trade_parts(): blocks = lax.all_to_all(blocks, mesh_axis, split_axis=0, concat_axis=0)]
    another operation x6 -> x0, local copies, waits for them, and re-layouts: 31.4 us -> none  [micro_step(): jnp.stack([d_queries, d_keys, d_values], axis=1).astype(jnp.bfloat16)]
where the time goes in v1:
time: 2020 us; the launch traced here: 2010 us
  waiting for transfers between devices  931 us (46%)
  matrix products  724 us (36%)
  other arithmetic  116 us (6%)
  local copies, waits for them, and re-layouts  101 us (5%)
  blocking collectives  91.2 us (5%)
  starting transfers between devices  30.8 us (2%)
    dot_general x8, matrix products, micro_step(): jnp.einsum('hqk,qhd->khd', d_scores, query_block, preferred_element_type=...  205 us
    dot_general x8, matrix products, micro_step(): jnp.einsum('hqk,khd->qhd', d_scores, keys_all, preferred_element_type=jnp...  185 us
    reduce_scatter x1, waiting for transfers between devices, body(): lax.psum_scatter(local_grads[4], 'shard', scatter_dimension=0, tiled=True)  163 us
    reduce_scatter x1, waiting for transfers between devices, body(): lax.psum_scatter(local_grads[6], 'shard', scatter_dimension=0, tiled=True)  163 us
    all_gather x1, waiting for transfers between devices, body(): lax.all_gather(inner_weight, 'shard', axis=0, tiled=True)  80.1 us
    all_gather x1, waiting for transfers between devices, body(): lax.all_gather(outer_weight, 'shard', axis=0, tiled=True)  79.8 us
    reduce_scatter x1, waiting for transfers between devices, body(): lax.psum_scatter(local_grads[0], 'shard', scatter_dimension=0, tiled=True)  70.7 us
    reduce_scatter x1, waiting for transfers between devices, body(): lax.psum_scatter(local_grads[2], 'shard', scatter_dimension=0, tiled=True)  70.6 us
  transfers between devices with their start and end apart: 21, of which 20 were waited for; matrix products, arithmetic and copies ran while one was open for 6% of the time, Pallas kernels for 0%

profile of v1, /device:TPU:0, one launch (start us, length us, event | category | flops | bytes accessed | tf_op | source)
XLA Modules:
  0.0 2014.6 jit_solution(15304259797592893149)
XLA Ops:
  41.4 26.0 %all-gather = bf16[8,1,384]{2,1,0:T(2,128)(2,1)S(1)} all-gather(bf16[1,1,384]{2,1,0:T(2,128)(2,1)S(1)} %reshape.334), channel_id=1, replica_groups=mesh['shard'=8,'seq'=4] {'shard'}, dimensions={0}, use_global_device_ids=true | all-gather | bytes 6912 | tf_op jit(solution)/shard_map/all_gather | solution.py:79
  67.5 28.6 %all-gather.10.cloned.1.call-done = bf16[768,768]{1,0:T(8,128)(2,1)} async-done(((bf16[96,768]{1,0:T(8,128)(2,1)}), bf16[768,768]{1,0:T(8,128)(2,1)}) %all-gather.10.cloned.1.call-update) | async-done | bytes 1179664 | tf_op jit(solution)/shard_map/all_gather | solution.py:75
  96.1 42.0 %all-gather.12.cloned.1.call-done = bf16[768,768]{1,0:T(8,128)(2,1)} async-done(((bf16[96,768]{1,0:T(8,128)(2,1)}), bf16[768,768]{1,0:T(8,128)(2,1)}) %all-gather.12.cloned.1.call-update) | async-done | bytes 1179664 | tf_op jit(solution)/shard_map/all_gather | solution.py:76
  141.4 38.6 %all-gather.14.cloned.1.call-done = bf16[768,768]{1,0:T(8,128)(2,1)} async-done(((bf16[96,768]{1,0:T(8,128)(2,1)}), bf16[768,768]{1,0:T(8,128)(2,1)}) %all-gather.14.cloned.1.call-update) | async-done | bytes 1179664 | tf_op jit(solution)/shard_map/all_gather | solution.py:77
  180.0 80.1 %all-gather.16.cloned.1.call-done = bf16[768,3072]{1,0:T(8,128)(2,1)} async-done(((bf16[96,3072]{1,0:T(8,128)(2,1)}), bf16[768,3072]{1,0:T(8,128)(2,1)}) %all-gather.16.cloned.1.call-update) | async-done | bytes 4718608 | tf_op jit(solution)/shard_map/all_gather | solution.py:78
  260.1 79.8 %all-gather.18.cloned.1.call-done = bf16[3072,768]{1,0:T(8,128)(2,1)} async-done(((bf16[384,768]{1,0:T(8,128)(2,1)}), bf16[3072,768]{1,0:T(8,128)(2,1)}) %all-gather.18.cloned.1.call-update) | async-done | bytes 4718608 | tf_op jit(solution)/shard_map/all_gather | solution.py:80
  339.8 994.1 %while.34 = (s32[]{:T(128)}, f32[768,2304]{1,0:T(8,128)}, f32[768,768]{1,0:T(8,128)}, f32[768,3072]{1,0:T(8,128)}, f32[3072]{0:T(1024)}, /*index=5*/f32[3072,768...) while((s32[]{:T(128)}, f32[768,2304]{1,0:T(8,128)}, ...), condition=%wide.region_30.31_spmd.clone, body=%wide.region_0.30_spmd.clone.sunk | while | flops 32022925312 | bytes 1231136000 | solution.py:275
  573.6 27.8 %fusion.480 = f32[3,64,2048]{2,1,0:T(8,128)} fusion(f32[3,512,2048]{2,1,0:T(8,128)} %fusion.479, f32[3,512,2048]{2,1,0:T(8,128)} %get-tuple-element.927, f32[3,512]{1,0:T(4,128)S(1)} %log_add_fusion.10, pred[512,2048]{1,0:T(8,128)(4,1)} %copy.117, bf16[2048,3,3,64]{0,3,2,1:T(8,128)(2,1)S(1)} %copy-done.1), kind=kOutput, calls=%fused_computation.47.clone.1 | convolution fusion | flops 437259776 | bytes 54214656 | tf_op jit(solution)/shard_map/while/body/eval_jaxpr/hqk,qhd->khd/dot_general | solution.py:238
  663.7 23.9 %fusion.488 = bf16[512,3,64]{0,2,1:T(8,128)(2,1)} fusion(f32[3,512,2048]{2,1,0:T(8,128)} %fusion.483, f32[3,512,2048]{2,1,0:T(8,128)} %get-tuple-element.921, f32[3,512]{1,0:T(4,128)S(1)} %log_add_fusion.8, pred[512,2048]{1,0:T(8,128)(4,1)} %copy.115, bf16[2048,3,3,64]{0,3,2,1:T(8,128)(2,1)S(1)} %copy-done.1), kind=kOutput, calls=%fused_computation.161.clone.1 | convolution fusion | flops 437358080 | bytes 53428224 | tf_op jit(solution)/shard_map/while/body/eval_jaxpr/hqk,khd->qhd/dot_general | solution.py:236
  687.6 24.0 %fusion.489 = bf16[512,3,64]{0,2,1:T(8,128)(2,1)} fusion(f32[3,512,2048]{2,1,0:T(8,128)} %fusion.481, f32[3,512,2048]{2,1,0:T(8,128)} %get-tuple-element.924, f32[3,512]{1,0:T(4,128)S(1)} %log_add_fusion.9, pred[512,2048]{1,0:T(8,128)(4,1)} %copy.116, bf16[2048,3,3,64]{0,3,2,1:T(8,128)(2,1)S(1)} %copy-done.1), kind=kOutput, calls=%fused_computation.160.clone.1 | convolution fusion | flops 437358080 | bytes 53428224 | tf_op jit(solution)/shard_map/while/body/eval_jaxpr/hqk,khd->qhd/dot_general | solution.py:236
  711.7 25.9 %fusion.482 = f32[3,64,2048]{2,1,0:T(8,128)} fusion(f32[3,64,2048]{2,1,0:T(8,128)} %fusion.480, f32[3,512,2048]{2,1,0:T(8,128)} %fusion.481, f32[3,512,2048]{2,1,0:T(8,128)} %get-tuple-element.924, f32[3,512]{1,0:T(4,128)S(1)} %log_add_fusion.9, pred[512,2048]{1,0:T(8,128)(4,1)} %copy.116, bf16[2048,3,3,64]{0,3,2,1:T(8,128)(2,1)S(1)} %copy-done.1), kind=kOutput, calls=%fused_computation.117.clone.1 | convolution fusion | flops 437652992 | bytes 55787520 | tf_op jit(solution)/shard_map/while/body/eval_jaxpr/hqk,qhd->khd/dot_general | solution.py:238
  737.5 26.4 %fusion.484 = f32[3,64,2048]{2,1,0:T(8,128)} fusion(f32[3,64,2048]{2,1,0:T(8,128)} %fusion.482, f32[3,512,2048]{2,1,0:T(8,128)} %fusion.483, f32[3,512,2048]{2,1,0:T(8,128)} %get-tuple-element.921, f32[3,512]{1,0:T(4,128)S(1)} %log_add_fusion.8, pred[512,2048]{1,0:T(8,128)(4,1)} %copy.115, bf16[2048,3,3,64]{0,3,2,1:T(8,128)(2,1)S(1)} %copy-done.1), kind=kOutput, calls=%fused_computation.116.clone.1 | convolution fusion | flops 437652992 | bytes 55787520 | tf_op jit(solution)/shard_map/while/body/eval_jaxpr/hqk,qhd->khd/dot_general | solution.py:238
  1068.1 27.8 %fusion.480 = f32[3,64,2048]{2,1,0:T(8,128)} fusion(f32[3,512,2048]{2,1,0:T(8,128)} %fusion.479, f32[3,512,2048]{2,1,0:T(8,128)} %get-tuple-element.927, f32[3,512]{1,0:T(4,128)S(1)} %log_add_fusion.10, pred[512,2048]{1,0:T(8,128)(4,1)} %copy.117, bf16[2048,3,3,64]{0,3,2,1:T(8,128)(2,1)S(1)} %copy-done.1), kind=kOutput, calls=%fused_computation.47.clone.1 | convolution fusion | flops 437259776 | bytes 54214656 | tf_op jit(solution)/shard_map/while/body/eval_jaxpr/hqk,qhd->khd/dot_general | solution.py:238
  1158.1 23.9 %fusion.488 = bf16[512,3,64]{0,2,1:T(8,128)(2,1)} fusion(f32[3,512,2048]{2,1,0:T(8,128)} %fusion.483, f32[3,512,2048]{2,1,0:T(8,128)} %get-tuple-element.921, f32[3,512]{1,0:T(4,128)S(1)} %log_add_fusion.8, pred[512,2048]{1,0:T(8,128)(4,1)} %copy.115, bf16[2048,3,3,64]{0,3,2,1:T(8,128)(2,1)S(1)} %copy-done.1), kind=kOutput, calls=%fused_computation.161.clone.1 | convolution fusion | flops 437358080 | bytes 53428224 | tf_op jit(solution)/shard_map/while/body/eval_jaxpr/hqk,khd->qhd/dot_general | solution.py:236
  1182.1 24.0 %fusion.489 = bf16[512,3,64]{0,2,1:T(8,128)(2,1)} fusion(f32[3,512,2048]{2,1,0:T(8,128)} %fusion.481, f32[3,512,2048]{2,1,0:T(8,128)} %get-tuple-element.924, f32[3,512]{1,0:T(4,128)S(1)} %log_add_fusion.9, pred[512,2048]{1,0:T(8,128)(4,1)} %copy.116, bf16[2048,3,3,64]{0,3,2,1:T(8,128)(2,1)S(1)} %copy-done.1), kind=kOutput, calls=%fused_computation.160.clone.1 | convolution fusion | flops 437358080 | bytes 53428224 | tf_op jit(solution)/shard_map/while/body/eval_jaxpr/hqk,khd->qhd/dot_general | solution.py:236
  1206.1 25.9 %fusion.482 = f32[3,64,2048]{2,1,0:T(8,128)} fusion(f32[3,64,2048]{2,1,0:T(8,128)} %fusion.480, f32[3,512,2048]{2,1,0:T(8,128)} %fusion.481, f32[3,512,2048]{2,1,0:T(8,128)} %get-tuple-element.924, f32[3,512]{1,0:T(4,128)S(1)} %log_add_fusion.9, pred[512,2048]{1,0:T(8,128)(4,1)} %copy.116, bf16[2048,3,3,64]{0,3,2,1:T(8,128)(2,1)S(1)} %copy-done.1), kind=kOutput, calls=%fused_computation.117.clone.1 | convolution fusion | flops 437652992 | bytes 55787520 | tf_op jit(solution)/shard_map/while/body/eval_jaxpr/hqk,qhd->khd/dot_general | solution.py:238
  1232.0 26.4 %fusion.484 = f32[3,64,2048]{2,1,0:T(8,128)} fusion(f32[3,64,2048]{2,1,0:T(8,128)} %fusion.482, f32[3,512,2048]{2,1,0:T(8,128)} %fusion.483, f32[3,512,2048]{2,1,0:T(8,128)} %get-tuple-element.921, f32[3,512]{1,0:T(4,128)S(1)} %log_add_fusion.8, pred[512,2048]{1,0:T(8,128)(4,1)} %copy.115, bf16[2048,3,3,64]{0,3,2,1:T(8,128)(2,1)S(1)} %copy-done.1), kind=kOutput, calls=%fused_computation.116.clone.1 | convolution fusion | flops 437652992 | bytes 55787520 | tf_op jit(solution)/shard_map/while/body/eval_jaxpr/hqk,qhd->khd/dot_general | solution.py:238
  1343.0 58.2 %reduce-scatter.13.cloned.1.call-done = f32[96,768]{1,0:T(8,128)} async-done(((f32[768,768]{1,0:T(8,128)}), f32[96,768]{1,0:T(8,128)}) %reduce-scatter.13.cloned.1.call-update) | async-done | bytes 294928 | tf_op jit(solution)/shard_map/reduce_scatter | solution.py:306
  1402.8 70.6 %reduce-scatter.11.cloned.1.call-done = f32[96,768]{1,0:T(8,128)} async-done(((f32[768,768]{1,0:T(8,128)}), f32[96,768]{1,0:T(8,128)}) %reduce-scatter.11.cloned.1.call-update) | async-done | bytes 294928 | tf_op jit(solution)/shard_map/reduce_scatter | solution.py:305
  1475.1 70.7 %reduce-scatter.7.cloned.1.call-done = f32[96,768]{1,0:T(8,128)} async-done(((f32[768,768]{1,0:T(8,128)}), f32[96,768]{1,0:T(8,128)}) %reduce-scatter.7.cloned.1.call-update) | async-done | bytes 294928 | tf_op jit(solution)/shard_map/reduce_scatter | solution.py:303
  1547.4 70.5 %reduce-scatter.9.cloned.1.call-done = f32[96,768]{1,0:T(8,128)} async-done(((f32[768,768]{1,0:T(8,128)}), f32[96,768]{1,0:T(8,128)}) %reduce-scatter.9.cloned.1.call-update) | async-done | bytes 294928 | tf_op jit(solution)/shard_map/reduce_scatter | solution.py:304
  1619.5 163.3 %reduce-scatter.15.cloned.1.call-done = f32[96,3072]{1,0:T(8,128)} async-done(((f32[768,3072]{1,0:T(8,128)}), f32[96,3072]{1,0:T(8,128)}) %reduce-scatter.15.cloned.1.call-update) | async-done | bytes 1179664 | tf_op jit(solution)/shard_map/reduce_scatter | solution.py:307
  1785.0 162.5 %reduce-scatter.17.cloned.1.call-done = f32[384,768]{1,0:T(8,128)} async-done(((f32[3072,768]{1,0:T(8,128)}), f32[384,768]{1,0:T(8,128)}) %reduce-scatter.17.cloned.1.call-update) | async-done | bytes 1179664 | tf_op jit(solution)/shard_map/reduce_scatter | solution.py:309
  1951.0 35.2 %all-reduce.9 = (bf16[3072]{0:T(1024)(128)(2,1)S(1)}, bf16[768]{0:T(1024)(128)(2,1)S(1)}, bf16[768]{0:T(1024)(128)(2,1)S(1)}, bf16[768]{0:T(1024)(128)(2,1)S(1)}, bf16[768]{0:T(1024)(128)(2,1)S(1)}) all-reduce(f32[3072]{0:T(1024)S(1)} %copy-done.25, f32[768]{0:T(1024)S(1)} %copy-done.39, ...), channel_id=7, replica_groups=mesh['shard'=8,'seq'=4] {'shard'}, use_global_device_ids=true, to_apply=%region_41.42.clone | all-reduce | flops 6144 | bytes 36864
  (494 shorter events, 811.4 us)
Async XLA Ops:
  7.2 60.3 %all-gather.8.cloned.1.call-start = ((), (), s32[]{:S(2)}) async-start(), calls=%async_computation.10 | async-start | bytes 1327104 | tf_op jit(solution)/shard_map/all_gather | solution.py:74
  7.9 88.2 %all-gather.10.cloned.1.call-start = ((), (), s32[]{:S(2)}) async-start(), calls=%async_computation.11 | async-start | bytes 1327104 | tf_op jit(solution)/shard_map/all_gather | solution.py:75
  8.7 129.4 %all-gather.12.cloned.1.call-start = ((), (), s32[]{:S(2)}) async-start(), calls=%async_computation.12 | async-start | bytes 1327104 | tf_op jit(solution)/shard_map/all_gather | solution.py:76
  9.4 170.6 %all-gather.14.cloned.1.call-start = ((), (), s32[]{:S(2)}) async-start(), calls=%async_computation.13 | async-start | bytes 1327104 | tf_op jit(solution)/shard_map/all_gather | solution.py:77
  10.0 250.1 %all-gather.16.cloned.1.call-start = ((), (), s32[]{:S(2)}) async-start(), calls=%async_computation.14 | async-start | bytes 5308416 | tf_op jit(solution)/shard_map/all_gather | solution.py:78
  10.6 329.3 %all-gather.18.cloned.1.call-start = ((), (), s32[]{:S(2)}) async-start(), calls=%async_computation.15 | async-start | bytes 5308416 | tf_op jit(solution)/shard_map/all_gather | solution.py:80
  11.1 1390.0 %reduce-scatter.13.cloned.1.call-start = ((), (), s32[]{:S(2)}) async-start(), calls=%async_computation.19 | async-start | bytes 2654208 | tf_op jit(solution)/shard_map/reduce_scatter | solution.py:306
  349.8 32.1 %all-to-all-start = ((bf16[512,3,4,192]{0,3,1,2:T(8,128)(2,1)}), bf16[512,3,4,192]{0,3,1,2:T(8,128)(2,1)S(1)}, u32[]{:S(2)}, u32[]{:S(2)}) async-start(bf16[512,3,4,192]{0,3,1,2:T(8,128)(2,1)} %copy.113), calls=%async_computation | async-start | bytes 4718592 | tf_op jit(solution)/shard_map/while/body/eval_jaxpr/all_to_all | solution.py:133
  474.4 15.1 all-to-all-start.1
  524.5 15.9 all-to-all-start.2
  791.1 32.2 %all-to-all-start.3 = ((bf16[4,512,3,1,192]{1,4,2,3,0:T(8,128)(2,1)}), bf16[4,512,3,1,192]{1,4,2,3,0:T(8,128)(2,1)S(1)}, u32[]{:S(2)}, u32[]{:S(2)}) async-start(bf16[4,512,3,1,192]{1,4,2,3,0:T(8,128)(2,1)} %pad_maximum_fusion.9), calls=%async_computation.3 | async-start | bytes 4718592 | tf_op jit(solution)/shard_map/while/body/eval_jaxpr/all_to_all | solution.py:16
  844.2 32.1 %all-to-all-start = ((bf16[512,3,4,192]{0,3,1,2:T(8,128)(2,1)}), bf16[512,3,4,192]{0,3,1,2:T(8,128)(2,1)S(1)}, u32[]{:S(2)}, u32[]{:S(2)}) async-start(bf16[512,3,4,192]{0,3,1,2:T(8,128)(2,1)} %copy.113), calls=%async_computation | async-start | bytes 4718592 | tf_op jit(solution)/shard_map/while/body/eval_jaxpr/all_to_all | solution.py:133
  968.9 15.1 all-to-all-start.1
  1018.9 15.9 all-to-all-start.2
  1285.5 32.2 %all-to-all-start.3 = ((bf16[4,512,3,1,192]{1,4,2,3,0:T(8,128)(2,1)}), bf16[4,512,3,1,192]{1,4,2,3,0:T(8,128)(2,1)S(1)}, u32[]{:S(2)}, u32[]{:S(2)}) async-start(bf16[4,512,3,1,192]{1,4,2,3,0:T(8,128)(2,1)} %pad_maximum_fusion.9), calls=%async_computation.3 | async-start | bytes 4718592 | tf_op jit(solution)/shard_map/while/body/eval_jaxpr/all_to_all | solution.py:16
  1334.0 139.4 %reduce-scatter.11.cloned.1.call-start = ((), (), s32[]{:S(2)}) async-start(), calls=%async_computation.18 | async-start | bytes 2654208 | tf_op jit(solution)/shard_map/reduce_scatter | solution.py:305
  1340.3 205.4 %reduce-scatter.7.cloned.1.call-start = ((), (), s32[]{:S(2)}) async-start(), calls=%async_computation.16 | async-start | bytes 2654208 | tf_op jit(solution)/shard_map/reduce_scatter | solution.py:303
  1341.0 276.8 %reduce-scatter.9.cloned.1.call-start = ((), (), s32[]{:S(2)}) async-start(), calls=%async_computation.17 | async-start | bytes 2654208 | tf_op jit(solution)/shard_map/reduce_scatter | solution.py:304
  1341.6 441.2 %reduce-scatter.15.cloned.1.call-start = ((), (), s32[]{:S(2)}) async-start(), calls=%async_computation.20 | async-start | bytes 10616832 | tf_op jit(solution)/shard_map/reduce_scatter | solution.py:307
  1342.4 605.1 %reduce-scatter.17.cloned.1.call-start = ((), (), s32[]{:S(2)}) async-start(), calls=%async_computation.21 | async-start | bytes 10616832 | tf_op jit(solution)/shard_map/reduce_scatter | solution.py:309
  1342.4 608.6 %copy-start.25 = (f32[3072]{0:T(1024)S(1)}, f32[3072]{0:T(1024)}, u32[]{:S(2)}) copy-start(f32[3072]{0:T(1024)} %get-tuple-element.1085) | copy-start | bytes 36868
  1342.4 608.6 %copy-start.30 = (f32[768]{0:T(1024)S(1)}, f32[768]{0:T(1024)}, u32[]{:S(2)}) copy-start(f32[768]{0:T(1024)} %get-tuple-element.1090) | copy-start | bytes 9220
  1342.4 608.6 %copy-start.33 = (f32[768]{0:T(1024)S(1)}, f32[768]{0:T(1024)}, u32[]{:S(2)}) copy-start(f32[768]{0:T(1024)} %get-tuple-element.1089) | copy-start | bytes 9220
  1342.9 653.9 %all-reduce.15.cloned.1.call-start = ((), (), s32[]{:S(2)}) async-start(), calls=%async_computation.22 | async-start | bytes 3538944 | tf_op jit(solution)/shard_map/psum | solution.py:316
  (95 other events, 2745.7 us)
Sparse Core Ops, SparseCore 0:
  10.2 43.8 all-gather.7
  56.2 39.8 all-gather.9
  98.3 39.8 all-gather.11
  140.1 39.8 all-gather.13
  182.0 78.0 all-gather.15
  262.1 77.6 all-gather.17
  1334.1 67.0 reduce-scatter.12
  1404.7 68.7 reduce-scatter.10
  1476.9 68.7 reduce-scatter.6
  1549.1 68.7 reduce-scatter.8
  1621.5 161.2 reduce-scatter.14
  1786.3 161.1 reduce-scatter.16
  1951.4 45.3 all-reduce.14
